TPU v7x, 512 devices: a whole 4x8x8 slice. The times are simulated.
512 devices in a mesh: group: 128 (over z, y, core), mp: 4 (over x).
Axes of the slice: x: 4, y: 8, z: 8, core: 2. Of those that a mesh axis runs over, the one named last changes fastest.
Arguments:
- observations: bfloat16 [16384, 512], P('group', 'mp'), may hold values from -6 to 6
- hidden_state: bfloat16 [8192, 1024], P('group', 'mp'), may hold values from -0.8984375 to 0.8984375
- cell_state: bfloat16 [8192, 1024], P('group', 'mp'), may hold values from -4 to 4
- arrival_order: int32 [8192], replicated, may hold values from 0 to 8191, as said below
- batch_counts: int32 [128], replicated, may hold values from 0 to 128, as said below
- input_weight: bfloat16 [512, 4, 1024], P(None, None, 'mp'), may hold values from -0.15625 to 0.15625
- state_weight: bfloat16 [1024, 4, 1024], P(None, None, 'mp'), may hold values from -0.15625 to 0.15625
- gate_bias: float32 [4, 1024], P(None, 'mp'), may hold values from -3 to 3
- head_weight: bfloat16 [1024, 2, 512], P(None, None, 'mp'), may hold values from -0.1875 to 0.1875
- head_bias: float32 [2, 512], P(None, 'mp'), may hold values from -3 to 3
- value_weight: bfloat16 [512, 1], P('mp'), may hold values from -0.25 to 0.25
- value_bias: float32 [1], replicated, may hold values from -3 to 3
- advantage_weight: bfloat16 [512, 18], P('mp'), may hold values from -0.25 to 0.25
- advantage_bias: float32 [18], replicated, may hold values from -3 to 3
Outputs:
- action_values: float32 [16384, 18], P('group')
- new_hidden: bfloat16 [8192, 1024], P('group', 'mp')
- new_cell: bfloat16 [8192, 1024], P('group', 'mp')
Inputs may be any that keep to these rules, and one draw needn't show every extreme that they name: `arrival_order`: A permutation: each actor id once. Positions starts[b] to starts[b] + batch_counts[b] - 1 hold the actors of batch b, where starts is the running sum of batch_counts. Of the actors of one owner (ids k * 64 to (k + 1) * 64 - 1), at most 1 lie in one batch. `batch_counts`: sums to 8192.
All inputs are finite; a program needn't handle non-finite values.
Results may differ from a plain program's by a relative error of at most 0.0019.
Values may be sent and summed in bfloat16 or wider, within the bound.
A program may use at most 64 MiB of HBM per device.

v0:
```python
import math

import jax
import jax.numpy as jnp
from jax import lax
from jax.sharding import PartitionSpec as P


def joined_along(blocks, dim):
    blocks = jnp.moveaxis(blocks, 0, dim)
    dims = blocks.shape
    return blocks.reshape(*dims[:dim], dims[dim] * dims[dim + 1], *dims[dim + 2 :])


def gather_together(arrays, axis, dims):
    flat = jnp.concatenate([a.reshape(-1) for a in arrays])
    lines, at, gathered = (lax.all_gather(flat, axis), 0, [])
    for a, dim in zip(arrays, dims):
        blocks = lines[:, at : at + a.size].reshape(-1, *a.shape)
        gathered.append(joined_along(blocks, dim))
        at += a.size
    return tuple(gathered)


def sent_to_all(x, axis):
    count = lax.axis_size(axis)
    return lax.all_to_all(jnp.broadcast_to(x[None], (count, *x.shape)), axis, 0, 0, tiled=True)


def gather_directly(x, axis, dim):
    return joined_along(sent_to_all(x, axis), dim)


def over_copies(x, axis):
    everything = sent_to_all(x, axis)
    return jnp.sum(everything, axis=0)


def together(arrays, axis):
    ends = [0]
    for a in arrays:
        ends.append(ends[-1] + a.size)
    total = over_copies(jnp.concatenate([a.ravel() for a in arrays]), axis)
    return tuple((total[b:e].reshape(a.shape) for a, b, e in zip(arrays, ends, ends[1:])))


def with_blank(table):
    blank = jnp.zeros((1,) + table.shape[1:], table.dtype)
    return jnp.concatenate([table, blank], axis=0)


def invert_slots(slot_of, capacity, missing):
    slots = jnp.arange(capacity, dtype=jnp.int32)
    items = jnp.arange(slot_of.shape[0], dtype=jnp.int32)
    hits = slot_of[None, :] == slots[:, None]
    found = jnp.any(hits, axis=1)
    picked = jnp.sum(jnp.where(hits, items[None, :], 0), axis=1)
    return jnp.where(found, picked, missing)


def owned_positions(arrival_order, own_index, per_owner):
    actor_total = arrival_order.shape[0]
    block_len = math.gcd(actor_total, 2048)
    block_count = actor_total // block_len
    local_ids = (arrival_order - own_index * per_owner).reshape(block_count, block_len)
    bases = jnp.arange(block_count, dtype=jnp.int32) * block_len
    owned = jnp.arange(per_owner, dtype=jnp.int32)
    offsets = jnp.arange(block_len, dtype=jnp.int32)

    def accumulate(total, pair):
        ids, base = pair
        hits = ids[None, :] == owned[:, None]
        found = jnp.sum(jnp.where(hits, (base + offsets)[None, :], 0), axis=1)
        return (total + found, None)

    result, _ = lax.scan(accumulate, jnp.zeros((per_owner,), jnp.int32), (local_ids, bases))
    return result


def advance(
    obs_part,
    hidden_part,
    cell_part,
    input_weight,
    state_weight,
    gate_bias,
    head_weight,
    head_bias,
    value_weight,
    value_bias,
    advantage_weight,
    advantage_bias,
):
    full_obs, full_hidden = gather_together((obs_part, hidden_part), "mp", (1, 1))
    row_count = obs_part.shape[0]
    unit_count = cell_part.shape[1]
    gate_values = jnp.dot(
        full_obs,
        input_weight.reshape(input_weight.shape[0], -1),
        preferred_element_type=jnp.float32,
    )
    gate_values = gate_values + jnp.dot(
        full_hidden,
        state_weight.reshape(state_weight.shape[0], -1),
        preferred_element_type=jnp.float32,
    )
    gate_values = gate_values.reshape(row_count, 4, unit_count) + gate_bias[None]
    cell_next = jax.nn.sigmoid(gate_values[:, 1]) * cell_part.astype(jnp.float32) + jax.nn.sigmoid(
        gate_values[:, 0]
    ) * jnp.tanh(gate_values[:, 2])
    hidden_next = (jax.nn.sigmoid(gate_values[:, 3]) * jnp.tanh(cell_next)).astype(jnp.bfloat16)
    whole_next = gather_directly(hidden_next, "mp", 1)
    head_units = head_weight.shape[2]
    stream = jnp.dot(
        whole_next,
        head_weight.reshape(head_weight.shape[0], -1),
        preferred_element_type=jnp.float32,
    )
    stream = jax.nn.relu(stream.reshape(row_count, 2, head_units) + head_bias[None]).astype(
        jnp.bfloat16
    )
    value_part = jnp.dot(stream[:, 0], value_weight, preferred_element_type=jnp.float32)
    advantage_part = jnp.dot(stream[:, 1], advantage_weight, preferred_element_type=jnp.float32)
    value_sum, advantage_sum = together((value_part, advantage_part), "mp")
    value_sum = value_sum + value_bias
    advantage_sum = advantage_sum + advantage_bias
    slot_values = value_sum + advantage_sum - jnp.mean(advantage_sum, axis=1, keepdims=True)
    return (hidden_next, cell_next.astype(jnp.bfloat16), slot_values)


def per_device(
    observations,
    hidden_state,
    cell_state,
    arrival_order,
    batch_counts,
    input_weight,
    state_weight,
    gate_bias,
    head_weight,
    head_bias,
    value_weight,
    value_bias,
    advantage_weight,
    advantage_bias,
):
    batch_total = batch_counts.shape[0]
    per_owner = hidden_state.shape[0]
    capacity = observations.shape[0]
    per_pair = capacity // batch_total
    own_index = lax.axis_index("group")
    batch_ends = jnp.cumsum(batch_counts)
    batch_starts = batch_ends - batch_counts
    own_positions = owned_positions(arrival_order, own_index, per_owner)
    own_batch = jnp.sum((own_positions[:, None] >= batch_ends[None, :]).astype(jnp.int32), axis=1)
    earlier = (own_batch[:, None] == own_batch[None, :]) & (
        own_positions[None, :] < own_positions[:, None]
    )
    own_rank = jnp.sum(earlier.astype(jnp.int32), axis=1)
    send_slot = own_batch * per_pair + own_rank
    send_index = invert_slots(send_slot, capacity, per_owner)
    local_slot = jnp.arange(capacity, dtype=jnp.int32)
    own_count = batch_counts[own_index]
    own_start = batch_starts[own_index]
    filled = local_slot < own_count
    slot_actor = lax.dynamic_slice_in_dim(
        jnp.concatenate([arrival_order, jnp.zeros((capacity,), jnp.int32)]), own_start, capacity
    )
    slot_owner = jnp.where(filled, slot_actor // per_owner, batch_total)
    before = (slot_owner[:, None] == slot_owner[None, :]) & (
        local_slot[None, :] < local_slot[:, None]
    )
    slot_rank = jnp.sum(before.astype(jnp.int32), axis=1)
    recv_slot = jnp.where(filled, slot_owner * per_pair + slot_rank, capacity)
    return_index = invert_slots(recv_slot, capacity, capacity)
    feature_count = observations.shape[1]
    obs_send = with_blank(observations)[return_index].reshape(batch_total, per_pair, feature_count)
    obs_got = lax.all_to_all(obs_send, "group", split_axis=0, concat_axis=0, tiled=True)
    obs_rows = obs_got.reshape(capacity, feature_count)[send_slot]
    new_hidden, new_cell, owner_values = advance(
        obs_rows,
        hidden_state,
        cell_state,
        input_weight,
        state_weight,
        gate_bias,
        head_weight,
        head_bias,
        value_weight,
        value_bias,
        advantage_weight,
        advantage_bias,
    )
    action_count = owner_values.shape[1]
    values_send = with_blank(owner_values)[send_index].reshape(batch_total, per_pair, action_count)
    values_got = lax.all_to_all(values_send, "group", split_axis=0, concat_axis=0, tiled=True)
    action_values = with_blank(values_got.reshape(capacity, action_count))[recv_slot]
    return (action_values, new_hidden, new_cell)


def solution(mesh):
    placed = (
        P("group", "mp"),
        P("group", "mp"),
        P("group", "mp"),
        P(),
        P(),
        P(None, None, "mp"),
        P(None, None, "mp"),
        P(None, "mp"),
        P(None, None, "mp"),
        P(None, "mp"),
        P("mp", None),
        P(),
        P("mp", None),
        P(),
    )
    return jax.shard_map(
        per_device,
        mesh=mesh,
        in_specs=placed,
        out_specs=(P("group", None), P("group", "mp"), P("group", "mp")),
        check_vma=False,
    )
```

profile of v0, /device:TPU:1, one launch (start us, length us, event | category | flops | bytes accessed | tf_op | source)
XLA Modules:
  0.0 103.2 jit_solution(16276334070150621702)
XLA Ops:
  0.7 0.9 copy.50
  1.5 0.2 reduce-window.8
  1.8 0.7 sub.23
  2.5 1.2 %dynamic_slice.17 = s32[1]{0:T(128)} dynamic-slice(s32[128]{0:T(128)} %param.20, s32[]{:T(128)S(6)} %select_n.90), dynamic_slice_sizes={1} | dynamic-slice | bytes 12 | tf_op jit(solution)/shard_map/dynamic_slice | solution.py:163
  3.7 0.6 dynamic_slice.18
  6.2 1.4 %compare_select_fusion.8 = s32[128]{0:T(128)S(1)} fusion(s32[]{:T(128)S(6)} %select_n.91, s32[8192]{0:T(1024)} %param.19, s32[]{:T(128)} %bitcast), kind=kLoop, calls=%fused_computation.77 | loop fusion | flops 2176 | bytes 33288 | tf_op jit(solution)/shard_map/jit(_where)/select_n | solution.py:169
  7.7 0.2 convert_reduce_fusion
  7.8 1.4 %compare_select_fusion = (s32[128]{0:T(128)S(1)}, s32[128]{0:T(128)S(1)}) fusion(s32[128]{0:T(128)S(1)} %convert_reduce_fusion, s32[]{:T(128)} %bitcast, s32[]{:T(128)S(6)} %select_n.91, s32[8192]{0:T(1024)} %param.19), kind=kLoop, calls=%fused_computation.68 | loop fusion | flops 2816 | bytes 34312 | tf_op jit(solution)/shard_map/select_n | solution.py:197
  9.5 0.8 concatenate.18
  10.3 0.7 gather_fusion
  11.0 0.7 copy.51
  11.7 18.4 %all-to-all-start = ((bf16[128,1,128]{2,1,0:T(2,128)(2,1)}), bf16[128,1,128]{2,1,0:T(2,128)(2,1)S(1)}, u32[]{:S(2)}, u32[]{:S(2)}) async-start(bf16[128,1,128]{2,1,0:T(2,128)(2,1)} %copy.51), calls=%async_computation | async-start | bytes 131072 | tf_op jit(solution)/shard_map/all_to_all | solution.py:178
  30.1 0.8 broadcast_subtract_fusion
  30.9 5.8 %while.11 = (s32[]{:T(128)}, s32[64]{0:T(128)S(1)}, s32[4,2048]{1,0:T(4,128)S(1)}, s32[4]{0:T(128)S(1)}, s32[]{:T(128)}, /*index=5*/s32[]{:T(128)}) while((s32[]{:T(128)}, s32[64]{0:T(128)S(1)}, s32[4,2048]{1,0:T(4,128)S(1)}, s32[4]{0:T(128)S(1)}, s32[]{:T(128)}, /*index=5*/s32[]{:T(128)}) %tuple.36), condition=%wide.region_6.7_spmd.clone, body=%wide.region_4.6_spmd.clone.sunk | while | flops 395331 | bytes 42083 | solution.py:76
  30.9 0.6 dynamic_slice.31
  31.5 0.6 iota_add_fusion.2
  32.2 0.2 select_reduce_fusion.4
  32.3 0.6 dynamic_slice.31
  32.9 0.6 iota_add_fusion.2
  33.8 0.6 dynamic_slice.31
  34.4 0.6 iota_add_fusion.2
  35.2 0.6 dynamic_slice.31
  35.8 0.6 iota_add_fusion.2
  36.7 0.2 convert_reduce_fusion.2
  36.9 0.2 convert_reduce_fusion.1
  37.2 0.6 select_reduce_fusion.2
  37.8 0.8 copy.65
  38.6 0.2 copy.67
  38.8 0.5 copy.69
  39.3 2.2 %all-to-all-done = bf16[128,1,128]{2,1,0:T(2,128)(2,1)S(1)} async-done(((bf16[128,1,128]{2,1,0:T(2,128)(2,1)}), bf16[128,1,128]{2,1,0:T(2,128)(2,1)S(1)}, u32[]{:S(2)}, u32[]{:S(2)}) %all-to-all-start) | async-done | bytes 32800 | tf_op jit(solution)/shard_map/all_to_all | solution.py:178
  41.6 0.6 gather_fusion.1
  42.2 9.6 %all-gather = bf16[98304]{0:T(1024)(128)(2,1)S(1)} all-gather(bf16[24576]{0:T(1024)(128)(2,1)S(1)} %pad_maximum_fusion), channel_id=2, replica_groups=mesh['group'=128,'mp'=4] {'mp'}, dimensions={0}, use_global_device_ids=true | all-gather | bytes 245760 | tf_op jit(solution)/shard_map/all_gather | solution.py:17
  52.0 0.3 fusion.7
  52.3 0.5 convolution_add_fusion
  52.9 0.7 fusion.34
  53.6 0.6 broadcast_in_dim.52
  54.3 3.4 %all-to-all-start.1 = ((bf16[4,64,256]{2,1,0:T(8,128)(2,1)}), bf16[4,64,256]{2,1,0:T(8,128)(2,1)S(1)}, u32[]{:S(2)}, u32[]{:S(2)}) async-start(bf16[4,64,256]{2,1,0:T(8,128)(2,1)} %broadcast_in_dim.52), calls=%async_computation.1 | async-start | bytes 262144 | tf_op jit(solution)/shard_map/all_to_all | solution.py:27
  57.8 0.2 copy.54
  58.0 4.5 %all-to-all-done.1 = bf16[4,64,256]{2,1,0:T(8,128)(2,1)S(1)} async-done(((bf16[4,64,256]{2,1,0:T(8,128)(2,1)}), bf16[4,64,256]{2,1,0:T(8,128)(2,1)S(1)}, u32[]{:S(2)}, u32[]{:S(2)}) %all-to-all-start.1) | async-done | bytes 131104 | tf_op jit(solution)/shard_map/all_to_all | solution.py:27
  62.7 0.3 fusion.6
  63.5 0.6 broadcast_in_dim.53
  64.1 3.3 %all-to-all-start.2 = ((f32[4,1,1216]{2,1,0:T(1,128)}), f32[4,1,1216]{2,1,0:T(1,128)S(1)}, u32[]{:S(2)}, u32[]{:S(2)}) async-start(f32[4,1,1216]{2,1,0:T(1,128)} %broadcast_in_dim.53), calls=%async_computation.2 | async-start | bytes 40960 | tf_op jit(solution)/shard_map/all_to_all | solution.py:27
  68.0 3.5 %all-to-all-done.2 = f32[4,1,1216]{2,1,0:T(1,128)S(1)} async-done(((f32[4,1,1216]{2,1,0:T(1,128)}), f32[4,1,1216]{2,1,0:T(1,128)S(1)}, u32[]{:S(2)}, u32[]{:S(2)}) %all-to-all-start.2) | async-done | bytes 19488 | tf_op jit(solution)/shard_map/all_to_all | solution.py:27
  72.0 1.2 %gather_fusion.2 = f32[128,18]{1,0:T(8,128)} fusion(f32[65,18]{1,0:T(8,128)S(1)} %concatenate.22, s32[1024]{0:T(1024)S(1)} %pad_clamp_fusion.1), kind=kCustom, calls=%fused_computation.2 | custom fusion | bytes 18944 | tf_op jit(solution)/shard_map/gather | solution.py:195
  73.3 17.1 %all-to-all-start.3 = ((f32[128,1,18]{2,1,0:T(1,128)}), f32[128,1,18]{2,1,0:T(1,128)S(1)}, u32[]{:S(2)}, u32[]{:S(2)}) async-start(f32[128,1,18]{2,1,0:T(1,128)} %bitcast.27), calls=%async_computation.3 | async-start | bytes 131072 | tf_op jit(solution)/shard_map/all_to_all | solution.py:196
  90.4 11.5 %all-to-all-done.3 = f32[128,1,18]{2,1,0:T(1,128)S(1)} async-done(((f32[128,1,18]{2,1,0:T(1,128)}), f32[128,1,18]{2,1,0:T(1,128)S(1)}, u32[]{:S(2)}, u32[]{:S(2)}) %all-to-all-start.3) | async-done | bytes 9248 | tf_op jit(solution)/shard_map/all_to_all | solution.py:196
  101.8 0.6 gather_fusion.3
  102.5 0.7 copy.58
  (70 shorter events, 2.5 us)
Async XLA Ops:
  0.6 62.3 %copy-start = (bf16[128,18]{0,1:T(8,128)(2,1)S(1)}, bf16[128,18]{0,1:T(8,128)(2,1)}, u32[]{:S(2)}) copy-start(bf16[128,18]{0,1:T(8,128)(2,1)} %param.28) | copy-start | bytes 13828
  0.6 37.9 %copy-start.2 = (bf16[512,4,256]{2,1,0:T(4,128)(2,1)S(1)}, bf16[512,4,256]{2,1,0:T(4,128)(2,1)}, u32[]{:S(2)}) copy-start(bf16[512,4,256]{2,1,0:T(4,128)(2,1)} %param.21) | copy-start | bytes 3145732
  11.7 29.9 %all-to-all-start = ((bf16[128,1,128]{2,1,0:T(2,128)(2,1)}), bf16[128,1,128]{2,1,0:T(2,128)(2,1)S(1)}, u32[]{:S(2)}, u32[]{:S(2)}) async-start(bf16[128,1,128]{2,1,0:T(2,128)(2,1)} %copy.51), calls=%async_computation | async-start | bytes 131072 | tf_op jit(solution)/shard_map/all_to_all | solution.py:178
  36.7 2.1 %copy-start.1 = (bf16[1024,4,256]{2,1,0:T(4,128)(2,1)S(1)}, bf16[1024,4,256]{2,1,0:T(4,128)(2,1)}, u32[]{:S(2)}) copy-start(bf16[1024,4,256]{2,1,0:T(4,128)(2,1)} %param.22) | copy-start | bytes 6291460
  52.0 0.9 copy-start.6
  52.0 0.9 copy-start.5
  52.3 5.4 %copy-start.10 = (s32[128]{0:T(128)S(1)}, s32[128]{0:T(128)}, u32[]{:S(2)}) copy-start(s32[128]{0:T(128)} %select_reduce_fusion.2) | copy-start | bytes 1540
  52.3 5.4 %copy-start.3 = (bf16[1024,2,128]{2,1,0:T(2,128)(2,1)S(1)}, bf16[1024,2,128]{2,1,0:T(2,128)(2,1)}, u32[]{:S(2)}) copy-start(bf16[1024,2,128]{2,1,0:T(2,128)(2,1)} %param.24) | copy-start | bytes 1572868
  52.8 9.9 %copy-start.8 = (f32[2,128]{1,0:T(2,128)S(1)}, f32[2,128]{1,0:T(2,128)}, u32[]{:S(2)}) copy-start(f32[2,128]{1,0:T(2,128)} %param.25) | copy-start | bytes 3076
  52.9 10.4 %copy-start.9 = (bf16[128,1]{0,1:T(2,128)(2,1)S(1)}, bf16[128,1]{0,1:T(2,128)(2,1)}, u32[]{:S(2)}) copy-start(bf16[128,1]{0,1:T(2,128)(2,1)} %param.26) | copy-start | bytes 772
  53.6 18.2 %copy-start.7 = (f32[18]{0:T(128)S(1)}, f32[18]{0:T(128)}, u32[]{:S(2)}) copy-start(f32[18]{0:T(128)} %param.29) | copy-start | bytes 220
  53.6 18.4 %copy-start.4 = (bf16[64,256]{1,0:T(8,128)(2,1)}, bf16[64,256]{1,0:T(8,128)(2,1)S(1)}, u32[]{:S(2)}) copy-start(bf16[64,256]{1,0:T(8,128)(2,1)S(1)} %fusion.27) | copy-start | bytes 98308
  54.3 8.2 %all-to-all-start.1 = ((bf16[4,64,256]{2,1,0:T(8,128)(2,1)}), bf16[4,64,256]{2,1,0:T(8,128)(2,1)S(1)}, u32[]{:S(2)}, u32[]{:S(2)}) async-start(bf16[4,64,256]{2,1,0:T(8,128)(2,1)} %broadcast_in_dim.52), calls=%async_computation.1 | async-start | bytes 262144 | tf_op jit(solution)/shard_map/all_to_all | solution.py:27
  64.1 7.5 %all-to-all-start.2 = ((f32[4,1,1216]{2,1,0:T(1,128)}), f32[4,1,1216]{2,1,0:T(1,128)S(1)}, u32[]{:S(2)}, u32[]{:S(2)}) async-start(f32[4,1,1216]{2,1,0:T(1,128)} %broadcast_in_dim.53), calls=%async_computation.2 | async-start | bytes 40960 | tf_op jit(solution)/shard_map/all_to_all | solution.py:27
  73.3 28.6 %all-to-all-start.3 = ((f32[128,1,18]{2,1,0:T(1,128)}), f32[128,1,18]{2,1,0:T(1,128)S(1)}, u32[]{:S(2)}, u32[]{:S(2)}) async-start(f32[128,1,18]{2,1,0:T(1,128)} %bitcast.27), calls=%async_computation.3 | async-start | bytes 131072 | tf_op jit(solution)/shard_map/all_to_all | solution.py:196
where the time goes:
time: 104 us; the launch traced here: 103 us
  starting transfers between devices  42.1 us (40%)
  waiting for transfers between devices  21.7 us (21%)
  local copies, waits for them, and re-layouts  14.2 us (14%)
  other arithmetic  10.4 us (10%)
  blocking collectives  9.59 us (9%)
  between operations  3.65 us (4%)
  matrix products  1.32 us (1%)
    all_to_all x1, starting transfers between devices, per_device(): lax.all_to_all(obs_send, 'group', split_axis=0, concat_axis=0, tiled=True)  18.4 us
    all_to_all x1, starting transfers between devices, per_device(): lax.all_to_all(values_send, 'group', split_axis=0, concat_axis=0, tiled=T...  17.1 us
    all_to_all x1, waiting for transfers between devices, per_device(): lax.all_to_all(values_send, 'group', split_axis=0, concat_axis=0, tiled=T...  11.5 us
    all_gather x1, blocking collectives, gather_together(): lines, at, gathered = (lax.all_gather(flat, axis), 0, [])  9.59 us
    all_to_all x2, waiting for transfers between devices, sent_to_all(): lax.all_to_all(jnp.broadcast_to(x[None], (count, *x.shape)), axis, 0, 0,...  8.04 us
    all_to_all x2, starting transfers between devices, sent_to_all(): lax.all_to_all(jnp.broadcast_to(x[None], (count, *x.shape)), axis, 0, 0,...  6.65 us
    add x4, other arithmetic, accumulate(): found = jnp.sum(jnp.where(hits, (base + offsets)[None, :], 0), axis=1)  2.59 us
    dynamic_slice x8, local copies, waits for them, and re-layouts, owned_positions(): lax.scan(accumulate, jnp.zeros((per_owner,), jnp.int32), (local_ids, bases))  2.4 us
  transfers between devices with their start and end apart: 4, of which 4 were waited for; matrix products, arithmetic and copies ran while one was open for 9% of the time, Pallas kernels for 0%

commit v1 on v0

v1 whole, which is shorter than its diff:
```python
import functools

import jax
import jax.numpy as jnp
from jax import lax
from jax.experimental import pallas as pl
from jax.experimental.pallas import tpu as pltpu
from jax.sharding import PartitionSpec as P

MESH = pl.DeviceIdType.MESH
F32 = jnp.float32
BF16 = jnp.bfloat16
NT = (((1,), (1,)), ((), ()))
TN = (((0,), (0,)), ((), ()))


def iota(shape, dim):
    return lax.broadcasted_iota(jnp.int32, shape, dim)


def dot(a, b, dims=(((1,), (0,)), ((), ()))):
    return lax.dot_general(a, b, dims, preferred_element_type=F32)


def pick(table, values, dims):
    high = values.astype(BF16)
    rest = values - high.astype(F32)
    mid = rest.astype(BF16)
    low = (rest - mid.astype(F32)).astype(BF16)
    return dot(table, high, dims) + dot(table, mid, dims) + dot(table, low, dims)


def step_kernel(
    groups,
    parts,
    obs_ref,
    hidden_ref,
    cell_ref,
    order_ref,
    counts_ref,
    wi_hbm,
    ws_hbm,
    gate_bias_ref,
    wh_hbm,
    head_bias_ref,
    value_weight_ref,
    value_bias_ref,
    adv_weight_ref,
    adv_bias_ref,
    q_out,
    hidden_out,
    cell_out,
    wi,
    ws,
    wh,
    obs_send,
    obs_recv,
    obs_all,
    hid_all,
    new_all,
    part_all,
    val_send,
    val_recv,
    wsem,
    gsem,
    xsem,
):
    me = lax.axis_index("group")
    x = lax.axis_index("mp")
    own = hidden_ref.shape[0]
    slots = obs_ref.shape[0]
    units = cell_ref.shape[1]
    head_units = head_bias_ref.shape[1]
    actions = adv_weight_ref.shape[1]

    barrier = pltpu.get_barrier_semaphore()

    def greet(k, carry):
        pl.semaphore_signal(
            barrier, inc=1, device_id=(lax.rem(me + k, groups), x), device_id_type=MESH
        )
        return carry

    lax.fori_loop(1, groups, greet, 0)
    for k in range(1, parts):
        pl.semaphore_signal(
            barrier, inc=1, device_id=(me, lax.rem(x + k, parts)), device_id_type=MESH
        )

    loads = [
        pltpu.make_async_copy(a, b, wsem.at[i])
        for i, (a, b) in enumerate(((ws_hbm, ws), (wi_hbm, wi), (wh_hbm, wh)))
    ]
    for load in loads:
        load.start()

    counts = jnp.broadcast_to(counts_ref[...], (8, groups))
    before = (iota((groups, groups), 0) < iota((groups, groups), 1)).astype(BF16)
    starts = dot(counts.astype(BF16), before).astype(jnp.int32)[0:1]
    ends = starts + counts[0:1]
    mine = iota((1, groups), 1) == me
    start = jnp.sum(jnp.where(mine, starts, 0), axis=1, keepdims=True)
    count = jnp.sum(jnp.where(mine, counts[0:1], 0), axis=1, keepdims=True)
    order = order_ref[...]
    rows = order.shape[0]
    first = start // 128
    row_of = iota((rows, 128), 0)
    owners, places = [], []
    for j in range(2):
        window = jnp.sum(jnp.where(row_of == first + j, order, 0), axis=0, keepdims=True)
        place = (first + j) * 128 + iota((1, 128), 1) - start
        real = (place >= 0) & (place < count)
        owners.append(jnp.where(real, window // own, -1))
        places.append(place)
    owner_hot = jnp.concatenate([iota((groups, 128), 0) == o for o in owners], axis=1)
    place_hot = jnp.concatenate([iota((slots, 128), 0) == p for p in places], axis=1)
    slot_of = dot(owner_hot.astype(BF16), place_hot.astype(BF16), NT).astype(BF16)
    obs_send[...] = dot(slot_of, obs_ref[...])

    local = order - me * own
    lane = iota((own, 128), 1)
    sub = iota((own, 128), 0)
    total = jnp.zeros((own, 128), jnp.int32)
    for r in range(rows):
        total = total + jnp.where(local[r : r + 1] == sub, lane + r * 128, 0)
    position = jnp.sum(total, axis=1, keepdims=True)
    batch_hot = ((position >= starts) & (position < ends)).astype(BF16)

    pl.semaphore_wait(barrier, groups + parts - 2)

    def to_group(src, dst, s):
        def send(k, carry):
            o = lax.rem(me + k, groups)
            pltpu.make_async_remote_copy(
                src_ref=src.at[pl.ds(o, 1)],
                dst_ref=dst.at[pl.ds(me, 1)],
                send_sem=gsem.at[s],
                recv_sem=gsem.at[s + 1],
                device_id=(o, x),
                device_id_type=MESH,
            ).start()
            return carry

        lax.fori_loop(1, groups, send, 0)
        dst[pl.ds(me, 1), :] = src[pl.ds(me, 1), :]

    def drain(ref, s):
        some = ref.at[pl.ds(0, groups - 1)]
        pltpu.make_async_copy(some, some, gsem.at[s]).wait()

    def to_parts(ref, s):
        copies = []
        for k in range(1, parts):
            copy = pltpu.make_async_remote_copy(
                src_ref=ref.at[x],
                dst_ref=ref.at[x],
                send_sem=xsem.at[s, 0, k],
                recv_sem=xsem.at[s, 1, k],
                device_id=(me, lax.rem(x + k, parts)),
                device_id_type=MESH,
            )
            copy.start()
            copies.append(copy)
        return copies

    to_group(obs_send, obs_recv, 0)
    hid_all[x] = hidden_ref[...]
    hid_copies = to_parts(hid_all, 0)
    for copy in hid_copies:
        copy.wait_recv()
    loads[0].wait()
    gates = jnp.zeros((own, 4 * units), F32)
    for p in range(parts):
        gates = gates + dot(hid_all[p], ws[p * units : (p + 1) * units])
    loads[1].wait()
    loads[2].wait()

    drain(obs_recv, 1)
    obs_all[x] = dot(batch_hot, obs_recv[...].astype(BF16)).astype(BF16)
    obs_copies = to_parts(obs_all, 1)
    for copy in obs_copies:
        copy.wait_recv()
    features = obs_ref.shape[1]
    for p in range(parts):
        gates = gates + dot(obs_all[p], wi[p * features : (p + 1) * features])
    gate = [
        gates[:, g * units : (g + 1) * units] + gate_bias_ref[g : g + 1, :] for g in range(4)
    ]
    cell = jax.nn.sigmoid(gate[1]) * cell_ref[...].astype(F32) + jax.nn.sigmoid(
        gate[0]
    ) * jnp.tanh(gate[2])
    hidden = (jax.nn.sigmoid(gate[3]) * jnp.tanh(cell)).astype(BF16)
    new_all[x] = hidden
    new_copies = to_parts(new_all, 2)
    hidden_out[...] = hidden
    cell_out[...] = cell.astype(BF16)
    for copy in new_copies:
        copy.wait_recv()
    stream = jnp.zeros((own, 2 * head_units), F32)
    for p in range(parts):
        stream = stream + dot(new_all[p], wh[p * units : (p + 1) * units])
    streams = [
        jnp.maximum(
            stream[:, i * head_units : (i + 1) * head_units] + head_bias_ref[i : i + 1, :], 0.0
        ).astype(BF16)
        for i in range(2)
    ]
    value = dot(streams[0], value_weight_ref[...])
    advantage = dot(streams[1], adv_weight_ref[...])
    part_all[x] = jnp.zeros((own, 128), F32)
    part_all[x, :, 0:actions] = (
        value + advantage - jnp.mean(advantage, axis=1, keepdims=True)
    )
    part_copies = to_parts(part_all, 3)
    for copy in part_copies:
        copy.wait_recv()
    bias = adv_bias_ref[...]
    bias = value_bias_ref[...] + bias - jnp.mean(bias, axis=1, keepdims=True)
    part_sum = part_all[0] + part_all[1] + part_all[2] + part_all[3]
    val_send[...] = jnp.zeros((groups, 128), F32)
    val_send[:, 0:actions] = pick(batch_hot, part_sum[:, 0:actions] + bias, TN)
    to_group(val_send, val_recv, 2)
    for copies in (hid_copies, obs_copies, new_copies, part_copies):
        for copy in copies:
            copy.wait_send()
    drain(obs_send, 0)
    drain(val_send, 2)
    drain(val_recv, 3)
    q_out[...] = pick(slot_of, val_recv[...], TN)[:, 0:actions]


def solution(mesh):
    groups, parts = mesh.shape["group"], mesh.shape["mp"]

    def per_device(
        observations,
        hidden_state,
        cell_state,
        arrival_order,
        batch_counts,
        input_weight,
        state_weight,
        gate_bias,
        head_weight,
        head_bias,
        value_weight,
        value_bias,
        advantage_weight,
        advantage_bias,
    ):
        slots, features = observations.shape
        own, units = hidden_state.shape
        head_units = head_bias.shape[1]
        actions = advantage_weight.shape[1]
        vmem = pl.BlockSpec(memory_space=pltpu.VMEM)
        hbm = pl.BlockSpec(memory_space=pl.ANY)
        dma = pltpu.SemaphoreType.DMA
        wi = input_weight.reshape(input_weight.shape[0], -1)
        ws = state_weight.reshape(state_weight.shape[0], -1)
        wh = head_weight.reshape(head_weight.shape[0], -1)
        return pl.pallas_call(
            functools.partial(step_kernel, groups, parts),
            name="acting_step",
            out_shape=(
                jax.ShapeDtypeStruct((slots, actions), F32),
                jax.ShapeDtypeStruct((own, units), BF16),
                jax.ShapeDtypeStruct((own, units), BF16),
            ),
            in_specs=[vmem] * 5 + [hbm, hbm, vmem, hbm] + [vmem] * 5,
            out_specs=(vmem,) * 3,
            scratch_shapes=[
                pltpu.VMEM(wi.shape, BF16),
                pltpu.VMEM(ws.shape, BF16),
                pltpu.VMEM(wh.shape, BF16),
                pltpu.VMEM((groups, features), F32),
                pltpu.VMEM((groups, features), F32),
                pltpu.VMEM((parts, own, features), BF16),
                pltpu.VMEM((parts, own, units), BF16),
                pltpu.VMEM((parts, own, units), BF16),
                pltpu.VMEM((parts, own, 128), F32),
                pltpu.VMEM((groups, 128), F32),
                pltpu.VMEM((groups, 128), F32),
                dma((3,)),
                dma((4,)),
                dma((4, 2, parts)),
            ],
            compiler_params=pltpu.CompilerParams(
                collective_id=0, has_side_effects=True, vmem_limit_bytes=32 * 2**20
            ),
        )(
            observations,
            hidden_state,
            cell_state,
            arrival_order.reshape(-1, 128),
            batch_counts.reshape(1, -1),
            wi,
            ws,
            gate_bias,
            wh,
            head_bias,
            value_weight,
            value_bias.reshape(1, 1),
            advantage_weight,
            advantage_bias.reshape(1, -1),
        )

    placed = (
        P("group", "mp"),
        P("group", "mp"),
        P("group", "mp"),
        P(),
        P(),
        P(None, None, "mp"),
        P(None, None, "mp"),
        P(None, "mp"),
        P(None, None, "mp"),
        P(None, "mp"),
        P("mp", None),
        P(),
        P("mp", None),
        P(),
    )
    return jax.shard_map(
        per_device,
        mesh=mesh,
        in_specs=placed,
        out_specs=(P("group", None), P("group", "mp"), P("group", "mp")),
        check_vma=False,
    )
```

time: 104 us -> 55.5 us (0.53)
  Pallas kernels: 0 us -> 46.8 us
  starting transfers between devices: 42.1 us -> 0 us
  waiting for transfers between devices: 21.7 us -> 0 us
  other arithmetic: 10.4 us -> 0 us
  blocking collectives: 9.59 us -> 0 us
  local copies, waits for them, and re-layouts: 14.2 us -> 6.83 us
  between operations: 3.65 us -> 1.54 us
  matrix products: 1.32 us -> 0 us
    pallas_call x0 -> x1, Pallas kernels: none -> 46.8 us  [per_device(): pl.pallas_call(functools.partial(step_kernel, groups, parts), name='actin...]
    all_to_all x4 -> x0, starting transfers between devices: 42.1 us -> none  [the longest x1 18.4 us: per_device(): lax.all_to_all(obs_send, 'group', split_axis=0, concat_axis=0, tiled=True)]
    all_to_all x4 -> x0, waiting for transfers between devices: 21.7 us -> none  [the longest x1 11.5 us: per_device(): lax.all_to_all(values_send, 'group', split_axis=0, concat_axis=0, tiled=T...]
    all_gather x1 -> x0, blocking collectives: 9.59 us -> none  [gather_together(): lines, at, gathered = (lax.all_gather(flat, axis), 0, [])]
    dynamic_slice x10 -> x0, local copies, waits for them, and re-layouts: 4.22 us -> none  [the longest x8 2.4 us: owned_positions(): lax.scan(accumulate, jnp.zeros((per_owner,), jnp.int32), (local_ids, bases))]
    unnamed x29 -> x25, local copies, waits for them, and re-layouts: 2.34 us -> 6.16 us
    gather x4 -> x0, local copies, waits for them, and re-layouts: 3.22 us -> none  [the longest x1 1.23 us: per_device(): with_blank(owner_values)[send_index]]
    select_n x5 -> x0, other arithmetic: 2.9 us -> none  [the longest x1 1.44 us: per_device(): with_blank(values_got.reshape(capacity, action_count))[recv_slot]]
  transfers between devices with their start and end apart: 4 -> 0, of which waited for: 4 -> 0; matrix products, arithmetic and copies ran while one was open for 9% -> 0% of each run, Pallas kernels for 0% -> 0%
where the time goes in v1:
time: 55.5 us; the launch traced here: 55.1 us
  Pallas kernels  46.8 us (84%)
  local copies, waits for them, and re-layouts  6.83 us (12%)
  between operations  1.54 us (3%)
    pallas_call x1, Pallas kernels, per_device(): pl.pallas_call(functools.partial(step_kernel, groups, parts), name='actin...  46.8 us
    unnamed x25, local copies, waits for them, and re-layouts  6.16 us

profile of v1, /device:TPU:1, one launch (start us, length us, event | category | flops | bytes accessed | tf_op | source)
XLA Modules:
  0.0 55.1 jit_solution(13937869087640139633)
XLA Ops:
  0.6 0.0 copy-start.8
  1.4 0.8 %copy.17.value_weight_ref = bf16[128,1]{1,0:T(8,128)(2,1)S(1)} copy(bf16[128,1]{0,1:T(2,128)(2,1)} %param.24) | data formatting | bytes 512 | tf_op args[10]
  2.2 0.8 %copy.18.adv_weight_ref = bf16[128,18]{1,0:T(8,128)(2,1)S(1)} copy(bf16[128,18]{0,1:T(8,128)(2,1)} %param.26) | data formatting | bytes 9216 | tf_op args[12]
  3.0 1.1 %copy.24 = bf16[128,8,2,128]{3,1,2,0:T(8,128)(2,1)S(1)} copy(bf16[128,8,2,128]{3,2,1,0:T(2,128)(2,1)} %bitcast.21) | data formatting | bytes 1048576
  4.2 1.4 %copy.20 = bf16[64,8,4,256]{3,1,2,0:T(8,128)(2,1)S(1)} copy(bf16[64,8,4,256]{3,2,1,0:T(4,128)(2,1)} %bitcast.20) | data formatting | bytes 2097152
  5.6 0.0 copy-done.8
  5.6 0.0 copy-start
  5.6 0.0 copy-start.1
  5.7 0.0 copy-start.2
  5.7 0.0 copy-start.3
  5.7 0.0 copy-start.4
  5.7 0.0 copy-start.5
  5.7 0.0 copy-start.6
  5.7 0.0 copy-start.7
  5.7 0.5 copy.21
  6.2 0.2 copy-done
  6.4 0.0 copy-done.1
  6.4 0.0 copy-done.2
  6.4 0.0 copy-done.3
  6.4 0.0 copy-done.4
  6.4 0.0 copy-done.5
  6.5 0.0 copy-done.6
  6.5 0.0 copy-done.7
  6.5 46.8 %acting_step.1 = (f32[128,18]{1,0:T(8,128)S(1)}, bf16[64,256]{1,0:T(8,128)(2,1)S(1)}, bf16[64,256]{1,0:T(8,128)(2,1)S(1)}) custom-call(bf16[128,128]{1,0:T(8,128)(2,1)S(1)} %copy-done, bf16[64,256]{1,0:T(8,128)(2,1)S(1)} %copy-done.1, bf16[64,256]{1,0:T(8,128)(2,1)S(1)} %copy-done.2, s32[64,128]{1,0:T(8,128)S(1)} %bitcast.16, s32[1,128]{1,0:T(1,128)S(1)} %bitcast.17, ...), custom_call_target="tpu_custom_call" | custom-call | tf_op jit(solution)/shard_map/acting_step/pallas_call | solution.py:261
  53.2 0.7 %copy.19 = f32[128,18]{0,1:T(8,128)} copy(f32[128,18]{1,0:T(8,128)S(1)} %get-tuple-element.3) | data formatting | bytes 18432 | tf_op jit(solution)/shard_map/acting_step/pallas_call | solution.py:261
  53.9 0.6 %copy.28 = bf16[64,256]{1,0:T(8,128)(2,1)} copy(bf16[64,256]{1,0:T(8,128)(2,1)S(1)} %get-tuple-element.10) | data formatting | bytes 65536
  54.5 0.6 %copy.29 = bf16[64,256]{1,0:T(8,128)(2,1)} copy(bf16[64,256]{1,0:T(8,128)(2,1)S(1)} %get-tuple-element.11) | data formatting | bytes 65536
Async XLA Ops:
  0.6 5.0 %copy-start.8 = (bf16[1024,4,256]{2,1,0:T(4,128)(2,1)S(1)}, bf16[1024,4,256]{2,1,0:T(4,128)(2,1)}, u32[]{:S(2)}) copy-start(bf16[1024,4,256]{2,1,0:T(4,128)(2,1)} %param.20) | copy-start | bytes 6291460
  5.6 0.8 %copy-start = (bf16[128,128]{1,0:T(8,128)(2,1)S(1)}, bf16[128,128]{1,0:T(8,128)(2,1)}, u32[]{:S(2)}) copy-start(bf16[128,128]{1,0:T(8,128)(2,1)} %obs_ref.1) | copy-start | bytes 98308
  5.6 0.8 %copy-start.1 = (bf16[64,256]{1,0:T(8,128)(2,1)S(1)}, bf16[64,256]{1,0:T(8,128)(2,1)}, u32[]{:S(2)}) copy-start(bf16[64,256]{1,0:T(8,128)(2,1)} %hidden_ref.1) | copy-start | bytes 98308
  5.7 0.8 %copy-start.2 = (bf16[64,256]{1,0:T(8,128)(2,1)S(1)}, bf16[64,256]{1,0:T(8,128)(2,1)}, u32[]{:S(2)}) copy-start(bf16[64,256]{1,0:T(8,128)(2,1)} %cell_ref.1) | copy-start | bytes 98308
  5.7 0.8 %copy-start.3 = (s32[8192]{0:T(1024)S(1)}, s32[8192]{0:T(1024)}, u32[]{:S(2)}) copy-start(s32[8192]{0:T(1024)} %param.17) | copy-start | bytes 98308
  5.7 0.8 %copy-start.4 = (f32[4,256]{1,0:T(4,128)S(1)}, f32[4,256]{1,0:T(4,128)}, u32[]{:S(2)}) copy-start(f32[4,256]{1,0:T(4,128)} %gate_bias_ref.1) | copy-start | bytes 12292
  5.7 0.8 %copy-start.5 = (f32[2,128]{1,0:T(2,128)S(1)}, f32[2,128]{1,0:T(2,128)}, u32[]{:S(2)}) copy-start(f32[2,128]{1,0:T(2,128)} %head_bias_ref.1) | copy-start | bytes 3076
  5.7 0.8 %copy-start.6 = (s32[128]{0:T(128)S(1)}, s32[128]{0:T(128)}, u32[]{:S(2)}) copy-start(s32[128]{0:T(128)} %param.18) | copy-start | bytes 1540
  5.7 0.7 %copy-start.7 = (f32[18]{0:T(128)S(1)}, f32[18]{0:T(128)}, u32[]{:S(2)}) copy-start(f32[18]{0:T(128)} %param.27) | copy-start | bytes 220

commit v2 on v1

v2 whole, which is shorter than its diff:
```python
import functools

import jax
import jax.numpy as jnp
from jax import lax
from jax.experimental import pallas as pl
from jax.experimental.pallas import tpu as pltpu
from jax.sharding import PartitionSpec as P

MESH = pl.DeviceIdType.MESH
F32 = jnp.float32
BF16 = jnp.bfloat16
NT = (((1,), (1,)), ((), ()))


def iota(shape, dim):
    return lax.broadcasted_iota(jnp.int32, shape, dim)


NN = (((1,), (0,)), ((), ()))


def dot(a, b, dims=NN):
    return lax.dot_general(a, b, dims, preferred_element_type=F32)


def pick(table, values):
    high = values.astype(BF16)
    rest = values - high.astype(F32)
    mid = rest.astype(BF16)
    low = (rest - mid.astype(F32)).astype(BF16)
    return dot(table, high) + dot(table, mid) + dot(table, low)


def regroup(src, dst):
    gates = dst.shape[0]
    block = 16

    def body(i, carry):
        at = pl.multiple_of(i * block, block)
        v = src[pl.ds(at, block)].astype(F32)
        t = pltpu.einshape("kjn->jkn", v).astype(BF16)
        for j in range(v.shape[1]):
            half, g = divmod(j, gates)
            dst[g, pl.ds(at, block), half * 128 : half * 128 + 128] = t[j]
        return carry

    lax.fori_loop(0, src.shape[0] // block, body, 0, unroll=4)


def step_kernel(
    groups,
    parts,
    peers,
    obs_in,
    hidden_in,
    cell_in,
    order_in,
    counts_in,
    wi_in,
    ws_in,
    gate_bias_in,
    wh_in,
    head_bias_in,
    value_weight_in,
    value_bias_in,
    adv_weight_in,
    adv_bias_in,
    q_out,
    hidden_out,
    cell_out,
    obs_ref,
    cell_ref,
    order_ref,
    counts_ref,
    gate_bias_ref,
    head_bias_ref,
    value_weight_ref,
    value_bias_ref,
    adv_weight_ref,
    adv_bias_ref,
    wi_raw,
    ws_raw,
    wh_raw,
    wi,
    ws,
    wh,
    obs_send,
    obs_recv,
    obs_all,
    hid_all,
    new_all,
    part_all,
    val_send,
    val_recv,
    batch_t,
    slot_t,
    lsem,
    gsem,
    xsem,
):
    me = lax.axis_index("group")
    x = lax.axis_index("mp")
    own = hidden_in.shape[0]
    slots = obs_ref.shape[0]
    features = obs_ref.shape[1]
    units = cell_ref.shape[1]
    head_units = head_bias_ref.shape[1]
    actions = adv_weight_ref.shape[0]

    loads = [
        pltpu.make_async_copy(src, dst, lsem.at[i])
        for i, (src, dst) in enumerate(
            (
                (order_in, order_ref),
                (counts_in, counts_ref),
                (obs_in, obs_ref),
                (ws_in, ws_raw),
                (hidden_in, hid_all.at[x]),
                (wi_in, wi_raw),
                (wh_in, wh_raw),
                (cell_in, cell_ref),
                (gate_bias_in, gate_bias_ref),
                (head_bias_in, head_bias_ref),
                (value_weight_in, value_weight_ref),
                (value_bias_in, value_bias_ref),
                (adv_weight_in, adv_weight_ref),
                (adv_bias_in, adv_bias_ref),
            )
        )
    ]
    for load in loads[:3]:
        load.start()
    barrier = pltpu.get_barrier_semaphore()
    others = [peer(me) for peer in peers]
    for other in others:
        pl.semaphore_signal(barrier, inc=1, device_id=(other, x), device_id_type=MESH)
    for k in range(1, parts):
        pl.semaphore_signal(
            barrier, inc=1, device_id=(me, lax.rem(x + k, parts)), device_id_type=MESH
        )
    for load in loads[3:]:
        load.start()

    loads[0].wait()
    loads[1].wait()
    counts = jnp.broadcast_to(counts_ref[...], (8, groups))
    before = (iota((groups, groups), 0) < iota((groups, groups), 1)).astype(BF16)
    starts = dot(counts.astype(BF16), before).astype(jnp.int32)[0:1]
    ends = starts + counts[0:1]
    mine = iota((1, groups), 1) == me
    start = jnp.sum(jnp.where(mine, starts, 0), axis=1, keepdims=True)
    count = jnp.sum(jnp.where(mine, counts[0:1], 0), axis=1, keepdims=True)
    order = order_ref[...]
    rows = order.shape[0]
    first = start // 128
    row_of = iota((rows, 128), 0)
    owners, places = [], []
    for j in range(2):
        window = jnp.sum(jnp.where(row_of == first + j, order, 0), axis=0, keepdims=True)
        place = (first + j) * 128 + iota((1, 128), 1) - start
        real = (place >= 0) & (place < count)
        owners.append(jnp.where(real, window // own, -1))
        places.append(place)
    owner_hot = jnp.concatenate([iota((groups, 128), 0) == o for o in owners], axis=1)
    place_hot = jnp.concatenate([iota((slots, 128), 0) == p for p in places], axis=1)
    owner_hot = owner_hot.astype(BF16)
    place_hot = place_hot.astype(BF16)
    slot_of = dot(owner_hot, place_hot, NT).astype(BF16)
    slot_t[...] = dot(place_hot, owner_hot, NT).astype(BF16)
    loads[2].wait()
    obs_send[...] = dot(slot_of, obs_ref[...])

    local = order - me * own
    lane = iota((own, 128), 1)
    sub = iota((own, 128), 0)
    total = jnp.zeros((own, 128), jnp.int32)
    for r in range(rows):
        total = total + jnp.where(local[r : r + 1] == sub, lane + r * 128, 0)
    position = jnp.sum(total, axis=1, keepdims=True)
    batch_hot = ((position >= starts) & (position < ends)).astype(F32)
    batch_t[...] = batch_hot.T.astype(BF16)
    batch_hot = batch_hot.astype(BF16)

    loads[3].wait()
    regroup(ws_raw, ws)

    pl.semaphore_wait(barrier, groups + parts - 2)

    def to_group(src, dst, s):
        for other in others:
            pltpu.make_async_remote_copy(
                src_ref=src.at[pl.ds(other, 1)],
                dst_ref=dst.at[pl.ds(me, 1)],
                send_sem=gsem.at[s],
                recv_sem=gsem.at[s + 1],
                device_id=(other, x),
                device_id_type=MESH,
            ).start()
        dst[pl.ds(me, 1), :] = src[pl.ds(me, 1), :]

    def drain(ref, s):
        some = ref.at[pl.ds(0, groups - 1)]
        pltpu.make_async_copy(some, some, gsem.at[s]).wait()

    def to_parts(ref, s):
        copies = []
        for k in (2, 1, 3):
            copy = pltpu.make_async_remote_copy(
                src_ref=ref.at[x],
                dst_ref=ref.at[x],
                send_sem=xsem.at[s, 0, k],
                recv_sem=xsem.at[s, 1, k],
                device_id=(me, lax.rem(x + k, parts)),
                device_id_type=MESH,
            )
            copy.start()
            copies.append(copy)
        return copies

    def over_parts(ref, copies, add):
        add(x, ref[x])
        for copy, k in zip(copies[1:] + copies[:1], (3, 1, 2)):
            copy.wait_recv()
            p = lax.rem(x + k, parts)
            add(p, ref[p])

    to_group(obs_send, obs_recv, 0)
    loads[4].wait()
    hid_copies = to_parts(hid_all, 0)
    loads[5].wait()
    regroup(wi_raw, wi)
    loads[6].wait()
    for i in range(2):
        wh[i] = wh_raw[:, i, :]
    for load in loads[7:]:
        load.wait()
    gate = [jnp.broadcast_to(gate_bias_ref[g : g + 1, :], (own, units)) for g in range(4)]

    def add_state(p, block):
        at = pl.ds(pl.multiple_of(p * units, units), units)
        for g in range(4):
            gate[g] = gate[g] + dot(block, ws[g, at, :])

    over_parts(hid_all, hid_copies, add_state)
    bias = adv_bias_ref[...]
    bias = value_bias_ref[...].reshape(1, 1) + bias - jnp.mean(bias, axis=1, keepdims=True)

    drain(obs_recv, 1)
    obs_all[x] = dot(batch_hot, obs_recv[...].astype(BF16)).astype(BF16)
    obs_copies = to_parts(obs_all, 1)

    def add_input(p, block):
        at = pl.ds(pl.multiple_of(p * features, features), features)
        for g in range(4):
            gate[g] = gate[g] + dot(block, wi[g, at, :])

    over_parts(obs_all, obs_copies, add_input)
    cell = jax.nn.sigmoid(gate[1]) * cell_ref[...].astype(F32) + jax.nn.sigmoid(
        gate[0]
    ) * jnp.tanh(gate[2])
    hidden = (jax.nn.sigmoid(gate[3]) * jnp.tanh(cell)).astype(BF16)
    new_all[x] = hidden
    new_copies = to_parts(new_all, 2)
    hidden_out[...] = hidden
    cell_out[...] = cell.astype(BF16)
    stream = [jnp.broadcast_to(head_bias_ref[i : i + 1, :], (own, head_units)) for i in range(2)]

    def add_head(p, block):
        at = pl.ds(pl.multiple_of(p * units, units), units)
        for i in range(2):
            stream[i] = stream[i] + dot(block, wh[i, at, :])

    over_parts(new_all, new_copies, add_head)
    stream = [jnp.maximum(s, 0.0).astype(BF16) for s in stream]
    value = jnp.sum(
        stream[0].astype(F32) * value_weight_ref[...].astype(F32), axis=1, keepdims=True
    )
    advantage = dot(stream[1], adv_weight_ref[...], NT)
    part_all[x] = jnp.zeros((own, 128), F32)
    part_all[x, :, 0:actions] = (
        value + advantage - jnp.mean(advantage, axis=1, keepdims=True)
    )
    part_copies = to_parts(part_all, 3)
    val_send[...] = jnp.zeros((groups, 128), F32)
    for copy in part_copies:
        copy.wait_recv()
    part_sum = part_all[0] + part_all[1] + part_all[2] + part_all[3]
    val_send[:, 0:actions] = pick(batch_t[...], part_sum[:, 0:actions] + bias)
    to_group(val_send, val_recv, 2)
    for copies in (hid_copies, obs_copies, new_copies, part_copies):
        for copy in copies:
            copy.wait_send()
    drain(obs_send, 0)
    drain(val_send, 2)
    drain(val_recv, 3)
    q_out[...] = pick(slot_t[...], val_recv[...])


def out_kernel(q_ref, hidden_ref, cell_ref, q_out, hidden_out, cell_out):
    hidden_out[...] = hidden_ref[...]
    cell_out[...] = cell_ref[...]
    q_out[...] = q_ref[...].T[0 : q_out.shape[0]]


def farthest_first(groups):
    side = 8
    ring = lambda d: min(d, side - d)
    moves = [(dz, dy, dc) for dz in range(side) for dy in range(side) for dc in range(2)]
    moves.sort(key=lambda m: -10 * (ring(m[0]) + ring(m[1])) - m[2])

    def peer(dz, dy, dc):
        def index(me):
            z, y, c = me // (2 * side), lax.rem(me // 2, side), lax.rem(me, 2)
            z, y, c = lax.rem(z + dz, side), lax.rem(y + dy, side), lax.rem(c + dc, 2)
            return (z * side + y) * 2 + c

        return index

    assert len(moves) == groups
    return [peer(*m) for m in moves if any(m)]


def solution(mesh):
    groups, parts = mesh.shape["group"], mesh.shape["mp"]

    def per_device(
        observations,
        hidden_state,
        cell_state,
        arrival_order,
        batch_counts,
        input_weight,
        state_weight,
        gate_bias,
        head_weight,
        head_bias,
        value_weight,
        value_bias,
        advantage_weight,
        advantage_bias,
    ):
        slots, features = observations.shape
        own, units = hidden_state.shape
        head_units = head_bias.shape[1]
        actions = advantage_weight.shape[1]
        vmem = pl.BlockSpec(memory_space=pltpu.VMEM)
        hbm = pl.BlockSpec(memory_space=pltpu.HBM)
        dma = pltpu.SemaphoreType.DMA

        def as_stored(w):
            return w.reshape(-1, 4, 2, 128).transpose(0, 2, 1, 3).reshape(-1, 8, 128)

        wi, ws = as_stored(input_weight), as_stored(state_weight)
        order = arrival_order.reshape(-1, 128)
        counts = batch_counts.reshape(1, -1)
        vw, aw, ab = value_weight.T, advantage_weight.T, advantage_bias.reshape(1, -1)
        like = lambda a: pltpu.VMEM(a.shape, a.dtype)
        q, new_hidden, new_cell = pl.pallas_call(
            functools.partial(step_kernel, groups, parts, farthest_first(groups)),
            name="acting_step",
            out_shape=(
                jax.ShapeDtypeStruct((slots, 128), F32),
                jax.ShapeDtypeStruct((own, units), BF16),
                jax.ShapeDtypeStruct((own, units), BF16),
            ),
            in_specs=[hbm] * 14,
            out_specs=(vmem,) * 3,
            scratch_shapes=[
                like(observations),
                like(cell_state),
                like(order),
                like(counts),
                like(gate_bias),
                like(head_bias),
                like(vw),
                like(value_bias),
                like(aw),
                like(ab),
                like(wi),
                like(ws),
                like(head_weight),
                pltpu.VMEM((4, wi.shape[0], units), BF16),
                pltpu.VMEM((4, ws.shape[0], units), BF16),
                pltpu.VMEM((2, head_weight.shape[0], head_units), BF16),
                pltpu.VMEM((groups, features), F32),
                pltpu.VMEM((groups, features), F32),
                pltpu.VMEM((parts, own, features), BF16),
                pltpu.VMEM((parts, own, units), BF16),
                pltpu.VMEM((parts, own, units), BF16),
                pltpu.VMEM((parts, own, 128), F32),
                pltpu.VMEM((groups, 128), F32),
                pltpu.VMEM((groups, 128), F32),
                pltpu.VMEM((groups, own), BF16),
                pltpu.VMEM((slots, groups), BF16),
                dma((14,)),
                dma((4,)),
                dma((4, 2, parts)),
            ],
            compiler_params=pltpu.CompilerParams(
                collective_id=0, has_side_effects=True, vmem_limit_bytes=60000000
            ),
        )(
            observations,
            hidden_state,
            cell_state,
            order,
            counts,
            wi,
            ws,
            gate_bias,
            head_weight,
            head_bias,
            vw,
            value_bias,
            aw,
            ab,
        )
        q, new_hidden, new_cell = pl.pallas_call(
            out_kernel,
            name="outputs",
            out_shape=(
                jax.ShapeDtypeStruct((actions, slots), F32),
                jax.ShapeDtypeStruct((own, units), BF16),
                jax.ShapeDtypeStruct((own, units), BF16),
            ),
            in_specs=[vmem] * 3,
            out_specs=(vmem,) * 3,
            compiler_params=pltpu.CompilerParams(vmem_limit_bytes=4 * 2**20),
        )(q, new_hidden, new_cell)
        return q.T, new_hidden, new_cell

    placed = (
        P("group", "mp"),
        P("group", "mp"),
        P("group", "mp"),
        P(),
        P(),
        P(None, None, "mp"),
        P(None, None, "mp"),
        P(None, "mp"),
        P(None, None, "mp"),
        P(None, "mp"),
        P("mp", None),
        P(),
        P("mp", None),
        P(),
    )
    return jax.shard_map(
        per_device,
        mesh=mesh,
        in_specs=placed,
        out_specs=(P("group", None), P("group", "mp"), P("group", "mp")),
        check_vma=False,
    )
```

time: 55.5 us -> 49.4 us (0.89)
  local copies, waits for them, and re-layouts: 6.83 us -> 2.35 us
  Pallas kernels: 46.8 us -> 45.5 us
    unnamed x25 -> x6, local copies, waits for them, and re-layouts: 6.16 us -> 2.35 us
    pallas_call x1 -> x2, Pallas kernels: 46.8 us -> 45.5 us  [the longest x1 44.8 us: per_device(): pl.pallas_call(functools.partial(step_kernel, groups, parts, farthest_fir...]
    pallas_call x1 -> x0, local copies, waits for them, and re-layouts: 0.68 us -> none  [per_device(): pl.pallas_call(functools.partial(step_kernel, groups, parts), name='actin...]
where the time goes in v2:
time: 49.4 us; the launch traced here: 49.1 us
  Pallas kernels  45.5 us (92%)
  local copies, waits for them, and re-layouts  2.35 us (5%)
  between operations  1.3 us (3%)
    pallas_call x1, Pallas kernels, per_device(): pl.pallas_call(functools.partial(step_kernel, groups, parts, farthest_fir...  44.8 us
    unnamed x6, local copies, waits for them, and re-layouts  2.35 us

profile of v2, /device:TPU:1, one launch (start us, length us, event | category | flops | bytes accessed | tf_op | source)
XLA Modules:
  0.0 49.1 jit_solution(9232086469027475373)
XLA Ops:
  1.3 44.8 %acting_step.1 = (f32[128,128]{1,0:T(8,128)}, bf16[64,256]{1,0:T(8,128)(2,1)}, bf16[64,256]{1,0:T(8,128)(2,1)}) custom-call(bf16[128,128]{1,0:T(8,128)(2,1)} %obs_in.1, bf16[64,256]{1,0:T(8,128)(2,1)} %hidden_in.1, bf16[64,256]{1,0:T(8,128)(2,1)} %cell_in.1, s32[64,128]{1,0:T(8,128)} %bitcast.18, s32[1,128]{1,0:T(1,128)} %bitcast.20, ...), custom_call_target="tpu_custom_call" | custom-call | tf_op jit(solution)/shard_map/acting_step/pallas_call | solution.py:359
  46.1 0.0 copy-start
  46.1 0.8 %copy-done = f32[128,128]{1,0:T(8,128)S(1)} copy-done((f32[128,128]{1,0:T(8,128)S(1)}, f32[128,128]{1,0:T(8,128)}, u32[]{:S(2)}) %copy-start) | copy-done | bytes 65560
  46.9 0.0 copy-start.1
  46.9 0.8 %copy-done.1 = bf16[64,256]{1,0:T(8,128)(2,1)S(1)} copy-done((bf16[64,256]{1,0:T(8,128)(2,1)S(1)}, bf16[64,256]{1,0:T(8,128)(2,1)}, u32[]{:S(2)}) %copy-start.1) | copy-done | bytes 32792
  47.7 0.0 copy-start.2
  47.7 0.8 %copy-done.2 = bf16[64,256]{1,0:T(8,128)(2,1)S(1)} copy-done((bf16[64,256]{1,0:T(8,128)(2,1)S(1)}, bf16[64,256]{1,0:T(8,128)(2,1)}, u32[]{:S(2)}) %copy-start.2) | copy-done | bytes 32792
  48.4 0.7 %outputs.1 = (f32[18,128]{1,0:T(8,128)}, bf16[64,256]{1,0:T(8,128)(2,1)}, bf16[64,256]{1,0:T(8,128)(2,1)}) custom-call(f32[128,128]{1,0:T(8,128)S(1)} %copy-done, bf16[64,256]{1,0:T(8,128)(2,1)S(1)} %copy-done.1, bf16[64,256]{1,0:T(8,128)(2,1)S(1)} %copy-done.2), custom_call_target="tpu_custom_call" | custom-call | tf_op jit(solution)/shard_map/outputs/pallas_call | solution.py:419
Async XLA Ops:
  46.1 0.8 %copy-start = (f32[128,128]{1,0:T(8,128)S(1)}, f32[128,128]{1,0:T(8,128)}, u32[]{:S(2)}) copy-start(f32[128,128]{1,0:T(8,128)} %get-tuple-element.9.q_ref) | copy-start | bytes 196612
  46.9 0.8 %copy-start.1 = (bf16[64,256]{1,0:T(8,128)(2,1)S(1)}, bf16[64,256]{1,0:T(8,128)(2,1)}, u32[]{:S(2)}) copy-start(bf16[64,256]{1,0:T(8,128)(2,1)} %get-tuple-element.10.hidden_ref) | copy-start | bytes 98308
  47.7 0.8 %copy-start.2 = (bf16[64,256]{1,0:T(8,128)(2,1)S(1)}, bf16[64,256]{1,0:T(8,128)(2,1)}, u32[]{:S(2)}) copy-start(bf16[64,256]{1,0:T(8,128)(2,1)} %get-tuple-element.11.cell_ref) | copy-start | bytes 98308

commit v3 on v2

--- a/solution.py
+++ b/solution.py
@@ -63,7 +63,7 @@
     wh_in,
     head_bias_in,
     value_weight_in,
-    value_bias_in,
+    value_bias_ref,
     adv_weight_in,
     adv_bias_in,
     q_out,
@@ -76,7 +76,6 @@
     gate_bias_ref,
     head_bias_ref,
     value_weight_ref,
-    value_bias_ref,
     adv_weight_ref,
     adv_bias_ref,
     wi_raw,
@@ -123,7 +122,6 @@
                 (gate_bias_in, gate_bias_ref),
                 (head_bias_in, head_bias_ref),
                 (value_weight_in, value_weight_ref),
-                (value_bias_in, value_bias_ref),
                 (adv_weight_in, adv_weight_ref),
                 (adv_bias_in, adv_bias_ref),
             )
@@ -182,9 +180,6 @@
     batch_t[...] = batch_hot.T.astype(BF16)
     batch_hot = batch_hot.astype(BF16)
 
-    loads[3].wait()
-    regroup(ws_raw, ws)
-
     pl.semaphore_wait(barrier, groups + parts - 2)
 
     def to_group(src, dst, s):
@@ -230,6 +225,8 @@
     hid_copies = to_parts(hid_all, 0)
     loads[5].wait()
     regroup(wi_raw, wi)
+    loads[3].wait()
+    regroup(ws_raw, ws)
     loads[6].wait()
     for i in range(2):
         wh[i] = wh_raw[:, i, :]
@@ -244,7 +241,7 @@
 
     over_parts(hid_all, hid_copies, add_state)
     bias = adv_bias_ref[...]
-    bias = value_bias_ref[...].reshape(1, 1) + bias - jnp.mean(bias, axis=1, keepdims=True)
+    bias = value_bias_ref[0] + bias - jnp.mean(bias, axis=1, keepdims=True)
 
     drain(obs_recv, 1)
     obs_all[x] = dot(batch_hot, obs_recv[...].astype(BF16)).astype(BF16)
@@ -345,6 +342,7 @@
         head_units = head_bias.shape[1]
         actions = advantage_weight.shape[1]
         vmem = pl.BlockSpec(memory_space=pltpu.VMEM)
+        smem = pl.BlockSpec(memory_space=pltpu.SMEM)
         hbm = pl.BlockSpec(memory_space=pltpu.HBM)
         dma = pltpu.SemaphoreType.DMA
 
@@ -364,7 +362,7 @@
                 jax.ShapeDtypeStruct((own, units), BF16),
                 jax.ShapeDtypeStruct((own, units), BF16),
             ),
-            in_specs=[hbm] * 14,
+            in_specs=[hbm] * 11 + [smem] + [hbm] * 2,
             out_specs=(vmem,) * 3,
             scratch_shapes=[
                 like(observations),
@@ -374,7 +372,6 @@
                 like(gate_bias),
                 like(head_bias),
                 like(vw),
-                like(value_bias),
                 like(aw),
                 like(ab),
                 like(wi),
@@ -393,28 +390,33 @@
                 pltpu.VMEM((groups, 128), F32),
                 pltpu.VMEM((groups, own), BF16),
                 pltpu.VMEM((slots, groups), BF16),
-                dma((14,)),
+                dma((13,)),
                 dma((4,)),
                 dma((4, 2, parts)),
             ],
             compiler_params=pltpu.CompilerParams(
-                collective_id=0, has_side_effects=True, vmem_limit_bytes=60000000
+                collective_id=0, has_side_effects=True, vmem_limit_bytes=32 * 2**20
             ),
         )(
-            observations,
-            hidden_state,
-            cell_state,
-            order,
-            counts,
-            wi,
-            ws,
-            gate_bias,
-            head_weight,
-            head_bias,
-            vw,
-            value_bias,
-            aw,
-            ab,
+            *(
+                a if a is value_bias else pltpu.with_memory_space_constraint(a, pltpu.HBM)
+                for a in (
+                    observations,
+                    hidden_state,
+                    cell_state,
+                    order,
+                    counts,
+                    wi,
+                    ws,
+                    gate_bias,
+                    head_weight,
+                    head_bias,
+                    vw,
+                    value_bias,
+                    aw,
+                    ab,
+                )
+            )
         )
         q, new_hidden, new_cell = pl.pallas_call(
             out_kernel,

time: 49.4 us -> 46.2 us (0.935)
  local copies, waits for them, and re-layouts: 2.35 us -> 0 us
  Pallas kernels: 45.5 us -> 44.8 us
    unnamed x6 -> x0, local copies, waits for them, and re-layouts: 2.35 us -> none
    pallas_call x1, Pallas kernels: 44.8 us -> 44.2 us  [per_device(): pl.pallas_call(functools.partial(step_kernel, groups, parts, farthest_fir...]
where the time goes in v3:
time: 46.2 us; the launch traced here: 46.1 us
  Pallas kernels  44.8 us (97%)
  between operations  1.29 us (3%)
    pallas_call x1, Pallas kernels, per_device(): pl.pallas_call(functools.partial(step_kernel, groups, parts, farthest_fir...  44.2 us

profile of v3, /device:TPU:1, one launch (start us, length us, event | category | flops | bytes accessed | tf_op | source)
XLA Modules:
  0.0 46.1 jit_solution(2578751278832951518)
XLA Ops:
  1.3 44.2 %acting_step.1 = (f32[128,128]{1,0:T(8,128)S(1)}, bf16[64,256]{1,0:T(8,128)(2,1)S(1)}, bf16[64,256]{1,0:T(8,128)(2,1)S(1)}) custom-call(bf16[128,128]{1,0:T(8,128)(2,1)} %obs_in.1, bf16[64,256]{1,0:T(8,128)(2,1)} %hidden_in.1, bf16[64,256]{1,0:T(8,128)(2,1)} %cell_in.1, s32[64,128]{1,0:T(8,128)} %bitcast.18, s32[1,128]{1,0:T(1,128)} %bitcast.20, ...), custom_call_target="tpu_custom_call" | custom-call | tf_op jit(solution)/shard_map/acting_step/pallas_call | solution.py:357
  45.4 0.7 %outputs.1 = (f32[18,128]{1,0:T(8,128)}, bf16[64,256]{1,0:T(8,128)(2,1)}, bf16[64,256]{1,0:T(8,128)(2,1)}) custom-call(f32[128,128]{1,0:T(8,128)S(1)} %get-tuple-element.9.q_ref, bf16[64,256]{1,0:T(8,128)(2,1)S(1)} %get-tuple-element.10.hidden_ref, bf16[64,256]{1,0:T(8,128)(2,1)S(1)} %get-tuple-element.11.cell_ref), custom_call_target="tpu_custom_call" | custom-call | tf_op jit(solution)/shard_map/outputs/pallas_call | solution.py:421

commit v4 on v3

--- a/solution.py
+++ b/solution.py
@@ -74,9 +74,9 @@
     order_ref,
     counts_ref,
     gate_bias_ref,
-    head_bias_ref,
-    value_weight_ref,
-    adv_weight_ref,
+    head_bias_all,
+    value_weight_all,
+    adv_weight_all,
     adv_bias_ref,
     wi_raw,
     ws_raw,
@@ -89,7 +89,6 @@
     obs_all,
     hid_all,
     new_all,
-    part_all,
     val_send,
     val_recv,
     batch_t,
@@ -97,6 +96,9 @@
     lsem,
     gsem,
     xsem,
+    ssem,
+    bsem,
+    fsem,
 ):
     me = lax.axis_index("group")
     x = lax.axis_index("mp")
@@ -104,8 +106,11 @@
     slots = obs_ref.shape[0]
     features = obs_ref.shape[1]
     units = cell_ref.shape[1]
-    head_units = head_bias_ref.shape[1]
-    actions = adv_weight_ref.shape[0]
+    head_units = head_bias_all.shape[2]
+    actions = adv_weight_all.shape[1]
+    core = lax.rem(me, 2)
+    sibling = me + 1 - 2 * core
+    half = wh_in.shape[0] // 2
 
     loads = [
         pltpu.make_async_copy(src, dst, lsem.at[i])
@@ -120,9 +125,9 @@
                 (wh_in, wh_raw),
                 (cell_in, cell_ref),
                 (gate_bias_in, gate_bias_ref),
-                (head_bias_in, head_bias_ref),
-                (value_weight_in, value_weight_ref),
-                (adv_weight_in, adv_weight_ref),
+                (head_bias_in, head_bias_all.at[x]),
+                (value_weight_in, value_weight_all.at[x]),
+                (adv_weight_in, adv_weight_all.at[x]),
                 (adv_bias_in, adv_bias_ref),
             )
         )
@@ -180,6 +185,9 @@
     batch_t[...] = batch_hot.T.astype(BF16)
     batch_hot = batch_hot.astype(BF16)
 
+    loads[6].wait()
+    for i in range(2):
+        wh[x, i] = wh_raw[:, i, :]
     pl.semaphore_wait(barrier, groups + parts - 2)
 
     def to_group(src, dst, s):
@@ -213,6 +221,61 @@
             copies.append(copy)
         return copies
 
+    def rows_at(first, count):
+        return pl.ds(pl.multiple_of(core * half + first, count), count)
+
+    whole = rows_at(0, half)
+    quarters = {1: rows_at(0, half // 2), 3: rows_at(half // 2, half // 2)}
+
+    def head_copy(p, at, sems, k, device):
+        block = wh.at[p, :, at]
+        copy = pltpu.make_async_remote_copy(
+            src_ref=block,
+            dst_ref=block,
+            send_sem=sems.at[0, k],
+            recv_sem=sems.at[1, k],
+            device_id=device,
+            device_id_type=MESH,
+        )
+        copy.start()
+        return copy
+
+    def spread():
+        return [
+            head_copy(x, whole, bsem.at[0], k, (me, lax.rem(x + k, parts))) for k in (1, 3)
+        ]
+
+    def relay(arrivals):
+        sent, handed = [], []
+        for copy, k in zip(arrivals, (1, 3)):
+            copy.wait_recv()
+            p = lax.rem(x + parts - k, parts)
+            sent.append(head_copy(p, quarters[k], bsem.at[1], k, (me, lax.rem(x + k, parts))))
+            handed.append(head_copy(p, whole, fsem.at[0], k, (sibling, x)))
+        return sent, handed
+
+    def spread_small():
+        copies = []
+        for i, (src, dst) in enumerate(
+            (
+                (head_bias_in, head_bias_all),
+                (value_weight_in, value_weight_all),
+                (adv_weight_in, adv_weight_all),
+            )
+        ):
+            for k in range(1, parts):
+                copy = pltpu.make_async_remote_copy(
+                    src_ref=src,
+                    dst_ref=dst.at[x],
+                    send_sem=ssem.at[i, 0, k],
+                    recv_sem=ssem.at[i, 1, k],
+                    device_id=(me, lax.rem(x + k, parts)),
+                    device_id_type=MESH,
+                )
+                copy.start()
+                copies.append(copy)
+        return copies
+
     def over_parts(ref, copies, add):
         add(x, ref[x])
         for copy, k in zip(copies[1:] + copies[:1], (3, 1, 2)):
@@ -223,13 +286,12 @@
     to_group(obs_send, obs_recv, 0)
     loads[4].wait()
     hid_copies = to_parts(hid_all, 0)
+    small_copies = spread_small()
+    near = spread()
     loads[5].wait()
     regroup(wi_raw, wi)
     loads[3].wait()
     regroup(ws_raw, ws)
-    loads[6].wait()
-    for i in range(2):
-        wh[i] = wh_raw[:, i, :]
     for load in loads[7:]:
         load.wait()
     gate = [jnp.broadcast_to(gate_bias_ref[g : g + 1, :], (own, units)) for g in range(4)]
@@ -243,9 +305,12 @@
     bias = adv_bias_ref[...]
     bias = value_bias_ref[0] + bias - jnp.mean(bias, axis=1, keepdims=True)
 
+    val_send[...] = jnp.zeros((groups, 128), F32)
+
     drain(obs_recv, 1)
     obs_all[x] = dot(batch_hot, obs_recv[...].astype(BF16)).astype(BF16)
     obs_copies = to_parts(obs_all, 1)
+    far, handed = relay(near)
 
     def add_input(p, block):
         at = pl.ds(pl.multiple_of(p * features, features), features)
@@ -261,31 +326,36 @@
     new_copies = to_parts(new_all, 2)
     hidden_out[...] = hidden
     cell_out[...] = cell.astype(BF16)
-    stream = [jnp.broadcast_to(head_bias_ref[i : i + 1, :], (own, head_units)) for i in range(2)]
+    for copy in far:
+        copy.wait_recv()
+    handed.append(head_copy(lax.rem(x + 2, parts), whole, fsem.at[0], 2, (sibling, x)))
+    for copy in small_copies:
+        copy.wait_recv()
+    for copy in handed:
+        copy.wait_recv()
+    stream = [
+        [jnp.broadcast_to(head_bias_all[p, i : i + 1, :], (own, head_units)) for p in range(parts)]
+        for i in range(2)
+    ]
 
     def add_head(p, block):
         at = pl.ds(pl.multiple_of(p * units, units), units)
         for i in range(2):
-            stream[i] = stream[i] + dot(block, wh[i, at, :])
+            for j in range(parts):
+                stream[i][j] = stream[i][j] + dot(block, wh[j, i, at, :])
 
     over_parts(new_all, new_copies, add_head)
-    stream = [jnp.maximum(s, 0.0).astype(BF16) for s in stream]
-    value = jnp.sum(
-        stream[0].astype(F32) * value_weight_ref[...].astype(F32), axis=1, keepdims=True
-    )
-    advantage = dot(stream[1], adv_weight_ref[...], NT)
-    part_all[x] = jnp.zeros((own, 128), F32)
-    part_all[x, :, 0:actions] = (
-        value + advantage - jnp.mean(advantage, axis=1, keepdims=True)
-    )
-    part_copies = to_parts(part_all, 3)
-    val_send[...] = jnp.zeros((groups, 128), F32)
-    for copy in part_copies:
-        copy.wait_recv()
-    part_sum = part_all[0] + part_all[1] + part_all[2] + part_all[3]
-    val_send[:, 0:actions] = pick(batch_t[...], part_sum[:, 0:actions] + bias)
+    stream = [[jnp.maximum(s, 0.0).astype(BF16) for s in part] for part in stream]
+    value = jnp.zeros((own, head_units), F32)
+    advantage = jnp.zeros((own, actions), F32)
+    for p in range(parts):
+        value = value + stream[0][p].astype(F32) * value_weight_all[p].astype(F32)
+        advantage = advantage + dot(stream[1][p], adv_weight_all[p], NT)
+    value = jnp.sum(value, axis=1, keepdims=True)
+    values = value + advantage - jnp.mean(advantage, axis=1, keepdims=True) + bias
+    val_send[:, 0:actions] = pick(batch_t[...], values)
     to_group(val_send, val_recv, 2)
-    for copies in (hid_copies, obs_copies, new_copies, part_copies):
+    for copies in (hid_copies, obs_copies, new_copies, small_copies, near, far, handed):
         for copy in copies:
             copy.wait_send()
     drain(obs_send, 0)
@@ -370,29 +440,29 @@
                 like(order),
                 like(counts),
                 like(gate_bias),
-                like(head_bias),
-                like(vw),
-                like(aw),
+                *(pltpu.VMEM((parts, *a.shape), a.dtype) for a in (head_bias, vw, aw)),
                 like(ab),
                 like(wi),
                 like(ws),
                 like(head_weight),
                 pltpu.VMEM((4, wi.shape[0], units), BF16),
                 pltpu.VMEM((4, ws.shape[0], units), BF16),
-                pltpu.VMEM((2, head_weight.shape[0], head_units), BF16),
+                pltpu.VMEM((parts, 2, head_weight.shape[0], head_units), BF16),
                 pltpu.VMEM((groups, features), F32),
                 pltpu.VMEM((groups, features), F32),
                 pltpu.VMEM((parts, own, features), BF16),
                 pltpu.VMEM((parts, own, units), BF16),
                 pltpu.VMEM((parts, own, units), BF16),
-                pltpu.VMEM((parts, own, 128), F32),
                 pltpu.VMEM((groups, 128), F32),
                 pltpu.VMEM((groups, 128), F32),
                 pltpu.VMEM((groups, own), BF16),
                 pltpu.VMEM((slots, groups), BF16),
                 dma((13,)),
                 dma((4,)),
-                dma((4, 2, parts)),
+                dma((3, 2, parts)),
+                dma((3, 2, parts)),
+                dma((2, 2, parts)),
+                dma((2, 2, parts)),
             ],
             compiler_params=pltpu.CompilerParams(
                 collective_id=0, has_side_effects=True, vmem_limit_bytes=32 * 2**20

time: 46.2 us -> 44.3 us (0.959)
  Pallas kernels: 44.8 us -> 42.9 us
    pallas_call x1, Pallas kernels: 44.2 us -> 42.2 us  [per_device(): pl.pallas_call(functools.partial(step_kernel, groups, parts, farthest_fir...]
where the time goes in v4:
time: 44.3 us; the launch traced here: 44.2 us
  Pallas kernels  42.9 us (97%)
  between operations  1.29 us (3%)
    pallas_call x1, Pallas kernels, per_device(): pl.pallas_call(functools.partial(step_kernel, groups, parts, farthest_fir...  42.2 us

profile of v4, /device:TPU:1, one launch (start us, length us, event | category | flops | bytes accessed | tf_op | source)
XLA Modules:
  0.0 44.2 jit_solution(7008133478596234888)
XLA Ops:
  1.3 42.2 %acting_step.1 = (f32[128,128]{1,0:T(8,128)S(1)}, bf16[64,256]{1,0:T(8,128)(2,1)S(1)}, bf16[64,256]{1,0:T(8,128)(2,1)S(1)}) custom-call(bf16[128,128]{1,0:T(8,128)(2,1)} %obs_in.1, bf16[64,256]{1,0:T(8,128)(2,1)} %hidden_in.1, bf16[64,256]{1,0:T(8,128)(2,1)} %cell_in.1, s32[64,128]{1,0:T(8,128)} %bitcast.18, s32[1,128]{1,0:T(1,128)} %bitcast.20, ...), custom_call_target="tpu_custom_call" | custom-call | tf_op jit(solution)/shard_map/acting_step/pallas_call | solution.py:427
  43.5 0.7 %outputs.1 = (f32[18,128]{1,0:T(8,128)}, bf16[64,256]{1,0:T(8,128)(2,1)}, bf16[64,256]{1,0:T(8,128)(2,1)}) custom-call(f32[128,128]{1,0:T(8,128)S(1)} %get-tuple-element.9.q_ref, bf16[64,256]{1,0:T(8,128)(2,1)S(1)} %get-tuple-element.10.hidden_ref, bf16[64,256]{1,0:T(8,128)(2,1)S(1)} %get-tuple-element.11.cell_ref), custom_call_target="tpu_custom_call" | custom-call | tf_op jit(solution)/shard_map/outputs/pallas_call | solution.py:491

commit v5 on v4

--- a/solution.py
+++ b/solution.py
@@ -283,11 +283,11 @@
             p = lax.rem(x + k, parts)
             add(p, ref[p])
 
+    near = spread()
     to_group(obs_send, obs_recv, 0)
     loads[4].wait()
     hid_copies = to_parts(hid_all, 0)
     small_copies = spread_small()
-    near = spread()
     loads[5].wait()
     regroup(wi_raw, wi)
     loads[3].wait()
@@ -301,7 +301,6 @@
         for g in range(4):
             gate[g] = gate[g] + dot(block, ws[g, at, :])
 
-    over_parts(hid_all, hid_copies, add_state)
     bias = adv_bias_ref[...]
     bias = value_bias_ref[0] + bias - jnp.mean(bias, axis=1, keepdims=True)
 
@@ -311,6 +310,7 @@
     obs_all[x] = dot(batch_hot, obs_recv[...].astype(BF16)).astype(BF16)
     obs_copies = to_parts(obs_all, 1)
     far, handed = relay(near)
+    over_parts(hid_all, hid_copies, add_state)
 
     def add_input(p, block):
         at = pl.ds(pl.multiple_of(p * features, features), features)

time: 44.3 us -> 43.5 us (0.982)
  Pallas kernels: 42.9 us -> 42 us
    pallas_call x1, Pallas kernels: 42.2 us -> 41.4 us  [per_device(): pl.pallas_call(functools.partial(step_kernel, groups, parts, farthest_fir...]
where the time goes in v5:
time: 43.5 us; the launch traced here: 43.3 us
  Pallas kernels  42 us (97%)
  between operations  1.29 us (3%)
    pallas_call x1, Pallas kernels, per_device(): pl.pallas_call(functools.partial(step_kernel, groups, parts, farthest_fir...  41.4 us

profile of v5, /device:TPU:1, one launch (start us, length us, event | category | flops | bytes accessed | tf_op | source)
XLA Modules:
  0.0 43.3 jit_solution(2333333952763634074)
XLA Ops:
  1.3 41.4 %acting_step.1 = (f32[128,128]{1,0:T(8,128)S(1)}, bf16[64,256]{1,0:T(8,128)(2,1)S(1)}, bf16[64,256]{1,0:T(8,128)(2,1)S(1)}) custom-call(bf16[128,128]{1,0:T(8,128)(2,1)} %obs_in.1, bf16[64,256]{1,0:T(8,128)(2,1)} %hidden_in.1, bf16[64,256]{1,0:T(8,128)(2,1)} %cell_in.1, s32[64,128]{1,0:T(8,128)} %bitcast.18, s32[1,128]{1,0:T(1,128)} %bitcast.20, ...), custom_call_target="tpu_custom_call" | custom-call | tf_op jit(solution)/shard_map/acting_step/pallas_call | solution.py:427
  42.7 0.7 %outputs.1 = (f32[18,128]{1,0:T(8,128)}, bf16[64,256]{1,0:T(8,128)(2,1)}, bf16[64,256]{1,0:T(8,128)(2,1)}) custom-call(f32[128,128]{1,0:T(8,128)S(1)} %get-tuple-element.9.q_ref, bf16[64,256]{1,0:T(8,128)(2,1)S(1)} %get-tuple-element.10.hidden_ref, bf16[64,256]{1,0:T(8,128)(2,1)S(1)} %get-tuple-element.11.cell_ref), custom_call_target="tpu_custom_call" | custom-call | tf_op jit(solution)/shard_map/outputs/pallas_call | solution.py:491
